TPU v7x, 32 devices: a whole 2x2x4 slice. The times are simulated.
32 devices in a mesh: groups: 2 (over x), tile: 16 (over z, y, core).
Axes of the slice: x: 2, y: 2, z: 4, core: 2. Of those that a mesh axis runs over, the one named last changes fastest.
Arguments:
- fine_nodes: bfloat16 [32768, 512], P(('groups', 'tile')), parts along dimension 0, may hold values from -6 to 6
- fine_table: int32 [16384, 6], P('tile'), may hold values from 0 to 16383, as said below
- mid_table: int32 [4096, 6], P('tile'), may hold values from 0 to 4095, as said below
- coarse_table: int32 [1024, 6], replicated, may hold values from 0 to 1023, as said below
- fine_parent: int32 [16384], P('tile'), may hold values from 0 to 4095, as said below
- mid_parent: int32 [4096], P('tile'), may hold values from 0 to 1023, as said below
- edge_self: bfloat16 [3, 512, 512], replicated, may hold values from -0.1875 to 0.1875
- edge_peer: bfloat16 [3, 512, 512], replicated, may hold values from -0.1875 to 0.1875
- edge_bias: float32 [3, 512], replicated, may hold values from -3 to 3
- node_self: bfloat16 [3, 512, 512], replicated, may hold values from -0.1875 to 0.1875
- node_message: bfloat16 [3, 512, 512], replicated, may hold values from -0.109375 to 0.109375
- node_bias: float32 [3, 512], replicated, may hold values from -3 to 3
- node_out: bfloat16 [3, 512, 512], replicated, may hold values from -0.25 to 0.25
- ascend_gain: float32 [2, 512], replicated, may hold values from 0.1 to 1.9
- down_self: bfloat16 [2, 512, 512], replicated, may hold values from -0.1875 to 0.1875
- down_parent: bfloat16 [2, 512, 512], replicated, may hold values from -0.1875 to 0.1875
- down_bias: float32 [2, 512], replicated, may hold values from -3 to 3
- down_out: bfloat16 [2, 512, 512], replicated, may hold values from -0.25 to 0.25
Outputs:
- fine_out: bfloat16 [32768, 512], P(('groups', 'tile')), parts along dimension 0
- mid_out: bfloat16 [8192, 512], P(('groups', 'tile')), parts along dimension 0
- coarse_out: bfloat16 [2048, 512], P(('groups', 'tile')), parts along dimension 0
There are 2 independent parts, one for each index of `groups`. A program takes and returns all parts, laid end to end along the dimension named above; an argument that names none is the same for every part. Nothing has to cross between parts.
Inputs may be any that keep to these rules, and one draw needn't show every extreme that they name: `fine_table`: fine node n is grid cell (n // 256, n % 256); each of its six neighbours lies in its own grid row or one of the two rows beside it, columns wrapping around. `mid_table`: Level-1 node p is cell (p // 128, p % 128); each neighbour lies in its own row or one of the two rows beside it, columns wrapping around. `coarse_table`: any level-2 nodes. `fine_parent`: the parent of fine cell (r, c) lies in level-1 row r // 2 - 1, r // 2 or r // 2 + 1. `mid_parent`: the parent of level-1 cell (r, c) lies in level-2 row r // 2 - 1, r // 2 or r // 2 + 1.
All inputs are finite; a program needn't handle non-finite values.
Results may differ from a plain program's by a relative error of at most 0.014.
Values may be sent and summed in bfloat16 or wider, within the bound.
A program may use at most 64 MiB of HBM per device.

v0:
```python
import jax
import jax.numpy as jnp
from jax import lax
from jax.sharding import PartitionSpec as P

COLS = 256


def with_halo(cells, sides, width):
    for axis, dim in sides:
        count = lax.axis_size(axis)
        ends = count - 1
        head = lax.slice_in_dim(cells, 0, width, axis=dim)
        tail = lax.slice_in_dim(cells, cells.shape[dim] - width, cells.shape[dim], axis=dim)
        cells = jnp.concatenate(
            [
                lax.ppermute(tail, axis, [(i, (i + 1) % count) for i in range(ends)]),
                cells,
                lax.ppermute(head, axis, [((i + 1) % count, i) for i in range(ends)]),
            ],
            axis=dim,
        )
    return cells


def gelu_tanh(values):
    return jax.nn.gelu(values, approximate=True)


def rim_rows(block_rows, col_count):
    feature_count = block_rows.shape[1]
    grid_rows = block_rows.reshape(block_rows.shape[0] // col_count, col_count, feature_count)
    padded = with_halo(grid_rows, (("tile", 0),), 1)
    return padded.reshape(-1, feature_count)


def finish_level(node_rows, summed, level_index, weights):
    node_self = weights[3]
    node_message = weights[4]
    node_bias = weights[5]
    node_out = weights[6]
    message = summed.astype(jnp.bfloat16)
    pre_act = jnp.dot(node_rows, node_self[level_index], preferred_element_type=jnp.float32)
    pre_act = (
        pre_act
        + jnp.dot(message, node_message[level_index], preferred_element_type=jnp.float32)
        + node_bias[level_index]
    )
    hidden = gelu_tanh(pre_act).astype(jnp.bfloat16)
    result = node_rows.astype(jnp.float32) + jnp.dot(
        hidden, node_out[level_index], preferred_element_type=jnp.float32
    )
    return result.astype(jnp.bfloat16)


def own_projection(node_rows, level_index, weights):
    return (
        jnp.dot(node_rows, weights[0][level_index], preferred_element_type=jnp.float32)
        + weights[2][level_index]
    )


def peer_projection(node_rows, level_index, weights):
    return jnp.dot(node_rows, weights[1][level_index], preferred_element_type=jnp.float32).astype(
        jnp.bfloat16
    )


def process_local(node_rows, neighbours, level_index, col_count, weights):
    own_proj = own_projection(node_rows, level_index, weights)
    extended = rim_rows(peer_projection(node_rows, level_index, weights), col_count)
    offset = lax.axis_index("tile") * node_rows.shape[0] - col_count
    local_ids = neighbours - offset
    summed = jnp.zeros(own_proj.shape, jnp.float32)
    for slot_index in range(6):
        fetched = extended[local_ids[:, slot_index]].astype(jnp.float32)
        summed = summed + gelu_tanh(own_proj + fetched)
    return finish_level(node_rows, summed, level_index, weights)


def ascend_local(children, parents, col_up, gain_vec):
    feature_count = children.shape[1]
    rows_up = children.shape[0] // (4 * col_up)
    span_rows = (rows_up + 2) * col_up
    offset = lax.axis_index("tile") * rows_up * col_up - col_up
    local_ids = parents - offset
    onehot = (local_ids[None, :] == jnp.arange(span_rows, dtype=jnp.int32)[:, None]).astype(
        jnp.bfloat16
    )
    partial_value = jnp.dot(onehot, children, preferred_element_type=jnp.float32)
    grid_rows = partial_value.reshape(rows_up + 2, col_up, feature_count)
    padded = with_halo(grid_rows.astype(jnp.bfloat16), (("tile", 0),), 1).astype(grid_rows.dtype)
    summed = grid_rows[1:-1]
    summed = summed.at[0].add(padded[0])
    summed = summed.at[-1].add(padded[-1])
    summed = summed.reshape(rows_up * col_up, feature_count)
    scale_inv = lax.rsqrt(jnp.mean(summed * summed, axis=1, keepdims=True) + 1e-05)
    return (summed * scale_inv * gain_vec).astype(jnp.bfloat16)


def descend_local(children, lifted_ext, parents, col_up, level_index, downs):
    down_self, down_parent, down_bias, down_out = downs
    rows_up = children.shape[0] // (4 * col_up)
    offset = lax.axis_index("tile") * rows_up * col_up - col_up
    fetched = lifted_ext[parents - offset].astype(jnp.float32)
    pre_act = (
        jnp.dot(children, down_self[level_index], preferred_element_type=jnp.float32)
        + fetched
        + down_bias[level_index]
    )
    hidden = gelu_tanh(pre_act).astype(jnp.bfloat16)
    result = children.astype(jnp.float32) + jnp.dot(
        hidden, down_out[level_index], preferred_element_type=jnp.float32
    )
    return result.astype(jnp.bfloat16)


def local(
    fine_nodes,
    fine_table,
    mid_table,
    coarse_table,
    fine_parent,
    mid_parent,
    edge_self,
    edge_peer,
    edge_bias,
    node_self,
    node_message,
    node_bias,
    node_out,
    ascend_gain,
    down_self,
    down_parent,
    down_bias,
    down_out,
):
    weights = (edge_self, edge_peer, edge_bias, node_self, node_message, node_bias, node_out)
    downs = (down_self, down_parent, down_bias, down_out)
    col_mid = COLS // 2
    col_low = COLS // 4
    fine_rows = process_local(fine_nodes, fine_table, 0, COLS, weights)
    mid_start = ascend_local(fine_rows, fine_parent, col_mid, ascend_gain[0])
    mid_rows = process_local(mid_start, mid_table, 1, col_mid, weights)
    coarse_start = ascend_local(mid_rows, mid_parent, col_low, ascend_gain[1])
    coarse_count = coarse_start.shape[0]
    peer_proj = peer_projection(coarse_start, 2, weights)
    own_proj = own_projection(coarse_start, 2, weights)
    my_table = lax.dynamic_slice_in_dim(
        coarse_table, lax.axis_index("tile") * coarse_count, coarse_count, 0
    )
    running = jnp.zeros(own_proj.shape, jnp.float32)
    fragment = lax.all_gather(peer_proj, "tile", axis=0, tiled=True)
    row_count = fragment.shape[0]
    for slot_index in range(6):
        where_ids = my_table[:, slot_index]
        inside = (where_ids >= 0) & (where_ids < row_count)
        fetched = fragment[jnp.clip(where_ids, 0, row_count - 1)].astype(jnp.float32)
        running = running + jnp.where(inside[:, None], gelu_tanh(own_proj + fetched), 0.0)
    coarse_final = finish_level(coarse_start, running, 2, weights)
    lifted_own = jnp.dot(coarse_final, down_parent[1], preferred_element_type=jnp.float32).astype(
        jnp.bfloat16
    )
    lifted_ext = rim_rows(lifted_own, col_low)
    mid_final = descend_local(mid_rows, lifted_ext, mid_parent, col_low, 1, downs)
    lifted_mid = rim_rows(
        jnp.dot(mid_final, down_parent[0], preferred_element_type=jnp.float32).astype(jnp.bfloat16),
        col_mid,
    )
    fine_final = descend_local(fine_rows, lifted_mid, fine_parent, col_mid, 0, downs)
    return (fine_final, mid_final, coarse_final)


def solution(mesh):
    placed = (
        P(("groups", "tile"), None),
        P("tile", None),
        P("tile", None),
        P(),
        P("tile"),
        P("tile"),
        P(),
        P(),
        P(),
        P(),
        P(),
        P(),
        P(),
        P(),
        P(),
        P(),
        P(),
        P(),
    )
    return jax.shard_map(
        local,
        mesh=mesh,
        in_specs=placed,
        out_specs=(
            P(("groups", "tile"), None),
            P(("groups", "tile"), None),
            P(("groups", "tile"), None),
        ),
        check_vma=False,
    )
```

profile of v0, /device:TPU:5, one launch (start us, length us, event | category | flops | bytes accessed | tf_op | source)
XLA Modules:
  0.0 196.6 jit_solution(9857290049073583987)
XLA Ops:
  7.3 2.1 %convolution_convert_fusion = bf16[1024,512]{1,0:T(8,128)(2,1)S(1)} fusion(bf16[1024,512]{1,0:T(8,128)(2,1)} %param.26, bf16[3,512,512]{2,1,0:T(8,128)(2,1)} %param.33), kind=kOutput, calls=%fused_computation.97 | convolution fusion | flops 537395200 | bytes 2621440 | tf_op jit(solution)/shard_map/dot_general | solution.py:64
  9.5 3.8 %collective-permute-start = (bf16[1,256,512]{2,1,0:T(8,128)(2,1)S(1)}, bf16[1,256,512]{2,1,0:T(8,128)(2,1)S(1)}, u32[]{:S(2)}, u32[]{:S(2)}) collective-permute-start(bf16[1,256,512]{2,1,0:T(8,128)(2,1)S(1)} %get-tuple-element.57), channel_id=1, source_target_pairs={{0,1},{1,2},{2,3},{3,4},{4,5},{5,6},{6,7},{7,8},{8,9},{9,10},{10,1... | collective-permute-start | bytes 786440 | tf_op jit(solution)/shard_map/ppermute | solution.py:17
  13.4 1.9 collective-permute-start.1
  15.5 3.1 %fusion.175 = f32[1024,512]{1,0:T(8,128)} fusion(bf16[1024,512]{1,0:T(8,128)(2,1)S(1)} %copy-done.3, bf16[3,512,512]{2,1,0:T(8,128)(2,1)} %param.35), kind=kOutput, calls=%fused_computation.221 | convolution fusion | flops 536870912 | bytes 3670016 | tf_op jit(solution)/shard_map/dot_general | solution.py:43
  18.7 3.2 %collective-permute-done.1 = bf16[1,256,512]{2,1,0:T(8,128)(2,1)S(1)} collective-permute-done((bf16[1,256,512]{2,1,0:T(8,128)(2,1)S(1)}, bf16[1,256,512]{2,1,0:T(8,128)(2,1)S(1)}, u32[]{:S(2)}, u32[]{:S(2)}) %collective-permute-start.1) | collective-permute-done | bytes 262176 | tf_op jit(solution)/shard_map/ppermute | solution.py:19
  21.9 0.2 pad_maximum_fusion
  22.1 5.1 %gather_fusion = bf16[1024,512]{1,0:T(8,128)(2,1)} fusion(bf16[1536,512]{1,0:T(8,128)(2,1)S(1)} %bitcast.201, s32[1024]{0:T(1024)S(1)} %broadcast_clamp_fusion.5), kind=kCustom, calls=%fused_computation | custom fusion | bytes 2101248 | tf_op jit(solution)/shard_map/gather | solution.py:76
  27.2 5.1 %gather_fusion.1 = bf16[1024,512]{1,0:T(8,128)(2,1)} fusion(bf16[1536,512]{1,0:T(8,128)(2,1)S(1)} %bitcast.202, s32[1024]{0:T(1024)S(1)} %broadcast_clamp_fusion.4), kind=kCustom, calls=%fused_computation.1 | custom fusion | bytes 2101248 | tf_op jit(solution)/shard_map/gather | solution.py:76
  32.3 5.1 %gather_fusion.2 = bf16[1024,512]{1,0:T(8,128)(2,1)} fusion(bf16[1536,512]{1,0:T(8,128)(2,1)S(1)} %bitcast.203, s32[1024]{0:T(1024)S(1)} %broadcast_clamp_fusion.3), kind=kCustom, calls=%fused_computation.2 | custom fusion | bytes 2101248 | tf_op jit(solution)/shard_map/gather | solution.py:76
  37.4 5.0 %gather_fusion.3 = bf16[1024,512]{1,0:T(8,128)(2,1)} fusion(bf16[1536,512]{1,0:T(8,128)(2,1)S(1)} %bitcast.204, s32[1024]{0:T(1024)S(1)} %broadcast_clamp_fusion.2), kind=kCustom, calls=%fused_computation.3 | custom fusion | bytes 2101248 | tf_op jit(solution)/shard_map/gather | solution.py:76
  42.4 5.1 %gather_fusion.4 = bf16[1024,512]{1,0:T(8,128)(2,1)} fusion(bf16[1536,512]{1,0:T(8,128)(2,1)S(1)} %bitcast.205, s32[1024]{0:T(1024)S(1)} %broadcast_clamp_fusion.1), kind=kCustom, calls=%fused_computation.4 | custom fusion | bytes 2101248 | tf_op jit(solution)/shard_map/gather | solution.py:76
  47.5 5.1 %gather_fusion.5 = bf16[1024,512]{1,0:T(8,128)(2,1)} fusion(bf16[1536,512]{1,0:T(8,128)(2,1)S(1)} %bitcast.206, s32[1024]{0:T(1024)S(1)} %broadcast_clamp_fusion), kind=kCustom, calls=%fused_computation.5 | custom fusion | bytes 2101248 | tf_op jit(solution)/shard_map/gather | solution.py:76
  52.5 10.0 %fusion.54 = bf16[1024,512]{1,0:T(8,128)(2,1)S(1)} fusion(f32[1024,512]{1,0:T(8,128)} %fusion.175, f32[512]{0:T(512)S(1)} %bitcast.245, bf16[1024,512]{1,0:T(8,128)(2,1)} %gather_fusion.5, bf16[1024,512]{1,0:T(8,128)(2,1)} %gather_fusion.4, bf16[1024,512]{1,0:T(8,128)(2,1)} %gather_fusion.3, bf16[1024,512]{1,0:T(8,128)(2,1)} %gather_fusion.2, ...), kind=kOutput, calls=%fused_computation.82 | convolution fusion | flops 1114636288 | bytes 11538432 | tf_op jit(solution)/shard_map/dot_general | solution.py:46
  62.5 1.7 add_convert_fusion.1
  64.3 0.7 fusion.343
  65.1 1.9 collective-permute-start.2
  67.0 2.6 %collective-permute-start.3 = (bf16[1,128,512]{2,1,0:T(8,128)(2,1)S(1)}, bf16[1,128,512]{2,1,0:T(8,128)(2,1)S(1)}, u32[]{:S(2)}, u32[]{:S(2)}) collective-permute-start(bf16[1,128,512]{2,1,0:T(8,128)(2,1)S(1)} %get-tuple-element.60), channel_id=1, source_target_pairs={{1,0},{2,1},{3,2},{4,3},{5,4},{6,5},{7,6},{8,7},{9,8},{10,9},{11,1... | collective-permute-start | bytes 393224 | tf_op jit(solution)/shard_map/ppermute | solution.py:19
  69.7 4.5 %collective-permute-done.3 = bf16[1,128,512]{2,1,0:T(8,128)(2,1)S(1)} collective-permute-done((bf16[1,128,512]{2,1,0:T(8,128)(2,1)S(1)}, bf16[1,128,512]{2,1,0:T(8,128)(2,1)S(1)}, u32[]{:S(2)}, u32[]{:S(2)}) %collective-permute-start.3) | collective-permute-done | bytes 131104 | tf_op jit(solution)/shard_map/ppermute | solution.py:19
  74.3 0.1 multiply_reduce_fusion
  74.4 0.1 multiply_convert_fusion
  74.5 1.5 convolution_convert_fusion.2
  76.0 0.3 fusion.160
  76.4 1.9 collective-permute-start.4
  78.3 2.4 %collective-permute-start.5 = (bf16[1,128,512]{2,1,0:T(8,128)(2,1)S(1)}, bf16[1,128,512]{2,1,0:T(8,128)(2,1)S(1)}, u32[]{:S(2)}, u32[]{:S(2)}) collective-permute-start(bf16[1,128,512]{2,1,0:T(8,128)(2,1)S(1)} %get-tuple-element.64), channel_id=1, source_target_pairs={{1,0},{2,1},{3,2},{4,3},{5,4},{6,5},{7,6},{8,7},{9,8},{10,9},{11,1... | collective-permute-start | bytes 393224 | tf_op jit(solution)/shard_map/ppermute | solution.py:19
  80.7 1.3 convolution_add_fusion.3
  82.1 0.8 fusion.163
  82.9 2.6 %collective-permute-done.5 = bf16[1,128,512]{2,1,0:T(8,128)(2,1)S(1)} collective-permute-done((bf16[1,128,512]{2,1,0:T(8,128)(2,1)S(1)}, bf16[1,128,512]{2,1,0:T(8,128)(2,1)S(1)}, u32[]{:S(2)}, u32[]{:S(2)}) %collective-permute-start.5) | collective-permute-done | bytes 131104 | tf_op jit(solution)/shard_map/ppermute | solution.py:19
  85.5 1.2 gather_fusion.10
  86.7 1.9 gather_fusion.6
  88.6 1.9 gather_fusion.7
  90.4 1.9 gather_fusion.8
  92.3 1.9 gather_fusion.9
  94.2 1.9 gather_fusion.11
  96.0 3.3 %fusion.66 = bf16[256,512]{1,0:T(8,128)(2,1)S(1)} fusion(f32[256,512]{1,0:T(8,128)S(1)} %fusion.160, bf16[3,512,512]{2,1,0:T(8,128)(2,1)} %param.38, bf16[3,512,512]{2,1,0:T(8,128)(2,1)} %param.36, bf16[256,512]{1,0:T(8,128)(2,1)} %fusion.163, f32[256,512]{1,0:T(8,128)S(1)} %convolution_add_fusion.3, bf16[256,512]{1,0:T(8,128)(2,1)} %gather_fusion.11, ...), kind=kOutput, calls=%fused_computation.103 | convolution fusion | flops 278921216 | bytes 4196352 | tf_op jit(solution)/shard_map/dot_general | solution.py:50
  99.3 0.2 fusion.344
  99.5 1.9 collective-permute-start.6
  101.5 2.4 %collective-permute-start.7 = (bf16[1,64,512]{2,1,0:T(8,128)(2,1)S(1)}, bf16[1,64,512]{2,1,0:T(8,128)(2,1)S(1)}, u32[]{:S(2)}, u32[]{:S(2)}) collective-permute-start(bf16[1,64,512]{2,1,0:T(8,128)(2,1)S(1)} %get-tuple-element.66), channel_id=1, source_target_pairs={{1,0},{2,1},{3,2},{4,3},{5,4},{6,5},{7,6},{8,7},{9,8},{10,9},{11,1... | collective-permute-start | bytes 196616 | tf_op jit(solution)/shard_map/ppermute | solution.py:19
  103.9 4.1 %collective-permute-done.7 = bf16[1,64,512]{2,1,0:T(8,128)(2,1)S(1)} collective-permute-done((bf16[1,64,512]{2,1,0:T(8,128)(2,1)S(1)}, bf16[1,64,512]{2,1,0:T(8,128)(2,1)S(1)}, u32[]{:S(2)}, u32[]{:S(2)}) %collective-permute-start.7) | collective-permute-done | bytes 65568 | tf_op jit(solution)/shard_map/ppermute | solution.py:19
  107.9 0.1 multiply_reduce_fusion.1
  108.1 0.1 multiply_convert_fusion.1
  108.2 1.9 convolution_convert_fusion.4
  110.1 0.1 constant_dynamic-slice_fusion
  110.3 0.2 fusion.151
  110.5 36.7 %all-gather.2.cloned.1.call-done = bf16[1024,512]{1,0:T(8,128)(2,1)} async-done(((bf16[64,512]{1,0:T(8,128)(2,1)}), bf16[1024,512]{1,0:T(8,128)(2,1)}) %all-gather.2.cloned.1.call-update) | async-done | bytes 1048592 | tf_op jit(solution)/shard_map/all_gather | solution.py:153
  147.2 2.2 %gather_fusion.12 = bf16[64,512]{1,0:T(8,128)(2,1)S(1)} fusion(bf16[1024,512]{1,0:T(8,128)(2,1)} %all-gather.2.cloned.1.call-done, s32[1024]{0:T(1024)S(1)} %get-tuple-element.112), kind=kCustom, calls=%fused_computation.12 | custom fusion | bytes 131328 | tf_op jit(solution)/shard_map/gather | solution.py:158
  149.3 2.1 %gather_fusion.13 = bf16[64,512]{1,0:T(8,128)(2,1)S(1)} fusion(bf16[1024,512]{1,0:T(8,128)(2,1)} %all-gather.2.cloned.1.call-done, s32[1024]{0:T(1024)S(1)} %get-tuple-element.111), kind=kCustom, calls=%fused_computation.13 | custom fusion | bytes 131328 | tf_op jit(solution)/shard_map/gather | solution.py:158
  151.4 2.1 %gather_fusion.14 = bf16[64,512]{1,0:T(8,128)(2,1)S(1)} fusion(bf16[1024,512]{1,0:T(8,128)(2,1)} %all-gather.2.cloned.1.call-done, s32[1024]{0:T(1024)S(1)} %get-tuple-element.110), kind=kCustom, calls=%fused_computation.14 | custom fusion | bytes 131328 | tf_op jit(solution)/shard_map/gather | solution.py:158
  153.5 0.7 gather_fusion.15
  154.2 0.7 gather_fusion.16
  154.9 0.7 gather_fusion.17
  155.6 1.7 fusion.297
  157.3 1.6 fusion.69
  158.9 0.2 fusion.70
  159.1 3.4 %collective-permute-start.8 = (bf16[1,64,512]{2,1,0:T(8,128)(2,1)S(1)}, bf16[1,64,512]{2,1,0:T(8,128)(2,1)S(1)}, u32[]{:S(2)}, u32[]{:S(2)}) collective-permute-start(bf16[1,64,512]{2,1,0:T(8,128)(2,1)S(1)} %fusion.70), channel_id=1, source_target_pairs={{0,1},{1,2},{2,3},{3,4},{4,5},{5,6},{6,7},{7,8},{8,9},{9,10},{10,1... | collective-permute-start | bytes 196616 | tf_op jit(solution)/shard_map/ppermute | solution.py:17
  162.6 1.9 collective-permute-start.9
  164.5 4.5 %collective-permute-done.9 = bf16[1,64,512]{2,1,0:T(8,128)(2,1)S(1)} collective-permute-done((bf16[1,64,512]{2,1,0:T(8,128)(2,1)S(1)}, bf16[1,64,512]{2,1,0:T(8,128)(2,1)S(1)}, u32[]{:S(2)}, u32[]{:S(2)}) %collective-permute-start.9) | collective-permute-done | bytes 65568 | tf_op jit(solution)/shard_map/ppermute | solution.py:19
  169.1 1.2 gather_fusion.18
  170.2 1.7 fusion.67
  171.9 0.3 convolution_convert_fusion.1
  172.3 1.9 collective-permute-start.10
  174.2 2.4 %collective-permute-start.11 = (bf16[1,128,512]{2,1,0:T(8,128)(2,1)S(1)}, bf16[1,128,512]{2,1,0:T(8,128)(2,1)S(1)}, u32[]{:S(2)}, u32[]{:S(2)}) collective-permute-start(bf16[1,128,512]{2,1,0:T(8,128)(2,1)S(1)} %get-tuple-element.62), channel_id=1, source_target_pairs={{1,0},{2,1},{3,2},{4,3},{5,4},{6,5},{7,6},{8,7},{9,8},{10,9},{11,1... | collective-permute-start | bytes 393224 | tf_op jit(solution)/shard_map/ppermute | solution.py:19
  176.6 4.8 %collective-permute-done.11 = bf16[1,128,512]{2,1,0:T(8,128)(2,1)S(1)} collective-permute-done((bf16[1,128,512]{2,1,0:T(8,128)(2,1)S(1)}, bf16[1,128,512]{2,1,0:T(8,128)(2,1)S(1)}, u32[]{:S(2)}, u32[]{:S(2)}) %collective-permute-start.11) | collective-permute-done | bytes 131104 | tf_op jit(solution)/shard_map/ppermute | solution.py:19
  181.4 4.0 %gather_fusion.19 = bf16[1024,512]{1,0:T(8,128)(2,1)S(1)} fusion(bf16[512,512]{1,0:T(8,128)(2,1)S(1)} %bitcast.213, s32[1024]{0:T(1024)S(1)} %get-tuple-element.51), kind=kCustom, calls=%fused_computation.19 | custom fusion | bytes 2101248 | tf_op jit(solution)/shard_map/gather | solution.py:105
  185.4 4.3 %add_convert_fusion = bf16[1024,512]{1,0:T(8,128)(2,1)} fusion(bf16[1024,512]{1,0:T(8,128)(2,1)} %copy-done.17, bf16[1024,512]{1,0:T(8,128)(2,1)S(1)} %gather_fusion.19, f32[512]{0:T(512)S(1)} %bitcast.244, bf16[2,512,512]{2,1,0:T(8,128)(2,1)S(1)} %copy-done.15, bf16[2,512,512]{2,1,0:T(8,128)(2,1)} %param.40), kind=kOutput, calls=%fused_computation.91 | convolution fusion | flops 1081606144 | bytes 5244928 | tf_op jit(solution)/shard_map/dot_general | solution.py:112
  (85 shorter events, 0.8 us)
Async XLA Ops:
  7.2 102.9 %copy-start = (s32[1024,6]{0,1:T(8,128)S(1)}, s32[1024,6]{0,1:T(8,128)}, u32[]{:S(2)}) copy-start(s32[1024,6]{0,1:T(8,128)} %param.29) | copy-start | bytes 73732
  7.2 8.3 %copy-start.3 = (bf16[1024,512]{1,0:T(8,128)(2,1)S(1)}, bf16[1024,512]{1,0:T(8,128)(2,1)}, u32[]{:S(2)}) copy-start(bf16[1024,512]{1,0:T(8,128)(2,1)} %param.26) | copy-start | bytes 3145732
  7.2 8.1 %copy-start.7 = (s32[1024,6]{0,1:T(8,128)S(1)}, s32[1024,6]{0,1:T(8,128)}, u32[]{:S(2)}) copy-start(s32[1024,6]{0,1:T(8,128)} %param.27) | copy-start | bytes 73732
  7.2 8.2 %copy-start.9 = (f32[3,512]{1,0:T(4,128)S(1)}, f32[3,512]{1,0:T(4,128)}, u32[]{:S(2)}) copy-start(f32[3,512]{1,0:T(4,128)} %param.37) | copy-start | bytes 18436
  7.2 139.9 %all-gather.2.cloned.1.call-start = ((), (), s32[]{:S(2)}) async-start(), calls=%async_computation | async-start | bytes 1114112 | tf_op jit(solution)/shard_map/all_gather | solution.py:153
  9.4 9.1 %copy-start.12 = (f32[2,512]{1,0:T(2,128)S(1)}, f32[2,512]{1,0:T(2,128)}, u32[]{:S(2)}) copy-start(f32[2,512]{1,0:T(2,128)} %param.39) | copy-start | bytes 12292
  9.5 9.1 %copy-start.11 = (s32[1024]{0:T(1024)S(1)}, s32[1024]{0:T(1024)}, u32[]{:S(2)}) copy-start(s32[1024]{0:T(1024)} %param.30) | copy-start | bytes 12292
  9.5 9.1 %copy-start.8 = (s32[256,6]{0,1:T(8,128)S(1)}, s32[256,6]{0,1:T(8,128)}, u32[]{:S(2)}) copy-start(s32[256,6]{0,1:T(8,128)} %param.28) | copy-start | bytes 18436
  9.5 9.2 %copy-start.14 = (s32[256]{0:T(256)S(1)}, s32[256]{0:T(256)}, u32[]{:S(2)}) copy-start(s32[256]{0:T(256)} %param.31) | copy-start | bytes 3076
  9.5 9.2 %copy-start.10 = (f32[3,512]{1,0:T(4,128)S(1)}, f32[3,512]{1,0:T(4,128)}, u32[]{:S(2)}) copy-start(f32[3,512]{1,0:T(4,128)} %param.34) | copy-start | bytes 18436
  9.5 9.2 %collective-permute-start = (bf16[1,256,512]{2,1,0:T(8,128)(2,1)S(1)}, bf16[1,256,512]{2,1,0:T(8,128)(2,1)S(1)}, u32[]{:S(2)}, u32[]{:S(2)}) collective-permute-start(bf16[1,256,512]{2,1,0:T(8,128)(2,1)S(1)} %get-tuple-element.57), channel_id=1, source_target_pairs={{0,1},{1,2},{2,3},{3,4},{4,5},{5,6},{6,7},{7,8},{8,9},{9,10},{10,1... | collective-permute-start | bytes 786440 | tf_op jit(solution)/shard_map/ppermute | solution.py:17
  13.4 8.6 %collective-permute-start.1 = (bf16[1,256,512]{2,1,0:T(8,128)(2,1)S(1)}, bf16[1,256,512]{2,1,0:T(8,128)(2,1)S(1)}, u32[]{:S(2)}, u32[]{:S(2)}) collective-permute-start(bf16[1,256,512]{2,1,0:T(8,128)(2,1)S(1)} %get-tuple-element.58), channel_id=1, source_target_pairs={{1,0},{2,1},{3,2},{4,3},{5,4},{6,5},{7,6},{8,7},{9,8},{10,9},{11,1... | collective-permute-start | bytes 786440 | tf_op jit(solution)/shard_map/ppermute | solution.py:19
  47.5 5.1 %copy-start.4 = (bf16[1024,512]{1,0:T(8,128)(2,1)S(1)}, bf16[1024,512]{1,0:T(8,128)(2,1)}, u32[]{:S(2)}) copy-start(bf16[1024,512]{1,0:T(8,128)(2,1)} %param.26) | copy-start | bytes 3145732
  64.3 5.4 %copy-start.17 = (bf16[1024,512]{1,0:T(8,128)(2,1)}, bf16[1024,512]{1,0:T(8,128)(2,1)S(1)}, u32[]{:S(2)}) copy-start(bf16[1024,512]{1,0:T(8,128)(2,1)S(1)} %add_convert_fusion.1) | copy-start | bytes 3145732
  65.1 4.6 %collective-permute-start.2 = (bf16[1,128,512]{2,1,0:T(8,128)(2,1)S(1)}, bf16[1,128,512]{2,1,0:T(8,128)(2,1)S(1)}, u32[]{:S(2)}, u32[]{:S(2)}) collective-permute-start(bf16[1,128,512]{2,1,0:T(8,128)(2,1)S(1)} %get-tuple-element.59), channel_id=1, source_target_pairs={{0,1},{1,2},{2,3},{3,4},{4,5},{5,6},{6,7},{7,8},{8,9},{9,10},{10,1... | collective-permute-start | bytes 393224 | tf_op jit(solution)/shard_map/ppermute | solution.py:17
  67.0 7.2 %collective-permute-start.3 = (bf16[1,128,512]{2,1,0:T(8,128)(2,1)S(1)}, bf16[1,128,512]{2,1,0:T(8,128)(2,1)S(1)}, u32[]{:S(2)}, u32[]{:S(2)}) collective-permute-start(bf16[1,128,512]{2,1,0:T(8,128)(2,1)S(1)} %get-tuple-element.60), channel_id=1, source_target_pairs={{1,0},{2,1},{3,2},{4,3},{5,4},{6,5},{7,6},{8,7},{9,8},{10,9},{11,1... | collective-permute-start | bytes 393224 | tf_op jit(solution)/shard_map/ppermute | solution.py:19
  74.2 1.8 copy-start.2
  76.4 6.5 %collective-permute-start.4 = (bf16[1,128,512]{2,1,0:T(8,128)(2,1)S(1)}, bf16[1,128,512]{2,1,0:T(8,128)(2,1)S(1)}, u32[]{:S(2)}, u32[]{:S(2)}) collective-permute-start(bf16[1,128,512]{2,1,0:T(8,128)(2,1)S(1)} %get-tuple-element.63), channel_id=1, source_target_pairs={{0,1},{1,2},{2,3},{3,4},{4,5},{5,6},{6,7},{7,8},{8,9},{9,10},{10,1... | collective-permute-start | bytes 393224 | tf_op jit(solution)/shard_map/ppermute | solution.py:17
  78.3 7.2 %collective-permute-start.5 = (bf16[1,128,512]{2,1,0:T(8,128)(2,1)S(1)}, bf16[1,128,512]{2,1,0:T(8,128)(2,1)S(1)}, u32[]{:S(2)}, u32[]{:S(2)}) collective-permute-start(bf16[1,128,512]{2,1,0:T(8,128)(2,1)S(1)} %get-tuple-element.64), channel_id=1, source_target_pairs={{1,0},{2,1},{3,2},{4,3},{5,4},{6,5},{7,6},{8,7},{9,8},{10,9},{11,1... | collective-permute-start | bytes 393224 | tf_op jit(solution)/shard_map/ppermute | solution.py:19
  99.3 11.0 %copy-start.13 = (f32[2,512]{1,0:T(2,128)S(1)}, f32[2,512]{1,0:T(2,128)}, u32[]{:S(2)}) copy-start(f32[2,512]{1,0:T(2,128)} %param.42) | copy-start | bytes 12292
  99.5 4.3 %collective-permute-start.6 = (bf16[1,64,512]{2,1,0:T(8,128)(2,1)S(1)}, bf16[1,64,512]{2,1,0:T(8,128)(2,1)S(1)}, u32[]{:S(2)}, u32[]{:S(2)}) collective-permute-start(bf16[1,64,512]{2,1,0:T(8,128)(2,1)S(1)} %get-tuple-element.65), channel_id=1, source_target_pairs={{0,1},{1,2},{2,3},{3,4},{4,5},{5,6},{6,7},{7,8},{8,9},{9,10},{10,1... | collective-permute-start | bytes 196616 | tf_op jit(solution)/shard_map/ppermute | solution.py:17
  101.5 6.5 %collective-permute-start.7 = (bf16[1,64,512]{2,1,0:T(8,128)(2,1)S(1)}, bf16[1,64,512]{2,1,0:T(8,128)(2,1)S(1)}, u32[]{:S(2)}, u32[]{:S(2)}) collective-permute-start(bf16[1,64,512]{2,1,0:T(8,128)(2,1)S(1)} %get-tuple-element.66), channel_id=1, source_target_pairs={{1,0},{2,1},{3,2},{4,3},{5,4},{6,5},{7,6},{8,7},{9,8},{10,9},{11,1... | collective-permute-start | bytes 196616 | tf_op jit(solution)/shard_map/ppermute | solution.py:19
  147.2 6.3 %copy-start.1 = (bf16[1024,512]{1,0:T(8,128)(2,1)S(1)}, bf16[1024,512]{1,0:T(8,128)(2,1)}, u32[]{:S(2)}) copy-start(bf16[1024,512]{1,0:T(8,128)(2,1)} %all-gather.2.cloned.1.call-done) | copy-start | bytes 3145732
  155.6 3.3 %copy-start.5 = (bf16[2,512,512]{2,1,0:T(8,128)(2,1)S(1)}, bf16[2,512,512]{2,1,0:T(8,128)(2,1)}, u32[]{:S(2)}) copy-start(bf16[2,512,512]{2,1,0:T(8,128)(2,1)} %param.41) | copy-start | bytes 3145732
  158.9 13.0 %copy-start.6 = (bf16[64,512]{1,0:T(8,128)(2,1)}, bf16[64,512]{1,0:T(8,128)(2,1)S(1)}, u32[]{:S(2)}) copy-start(bf16[64,512]{1,0:T(8,128)(2,1)S(1)} %fusion.69) | copy-start | bytes 196612
  158.9 11.3 %copy-start.15 = (bf16[2,512,512]{2,1,0:T(8,128)(2,1)S(1)}, bf16[2,512,512]{2,1,0:T(8,128)(2,1)}, u32[]{:S(2)}) copy-start(bf16[2,512,512]{2,1,0:T(8,128)(2,1)} %param.43) | copy-start | bytes 3145732
  159.1 5.4 %collective-permute-start.8 = (bf16[1,64,512]{2,1,0:T(8,128)(2,1)S(1)}, bf16[1,64,512]{2,1,0:T(8,128)(2,1)S(1)}, u32[]{:S(2)}, u32[]{:S(2)}) collective-permute-start(bf16[1,64,512]{2,1,0:T(8,128)(2,1)S(1)} %fusion.70), channel_id=1, source_target_pairs={{0,1},{1,2},{2,3},{3,4},{4,5},{5,6},{6,7},{7,8},{8,9},{9,10},{10,1... | collective-permute-start | bytes 196616 | tf_op jit(solution)/shard_map/ppermute | solution.py:17
  162.6 6.5 %collective-permute-start.9 = (bf16[1,64,512]{2,1,0:T(8,128)(2,1)S(1)}, bf16[1,64,512]{2,1,0:T(8,128)(2,1)S(1)}, u32[]{:S(2)}, u32[]{:S(2)}) collective-permute-start(bf16[1,64,512]{2,1,0:T(8,128)(2,1)S(1)} %fusion.70), channel_id=1, source_target_pairs={{1,0},{2,1},{3,2},{4,3},{5,4},{6,5},{7,6},{8,7},{9,8},{10,9},{11,1... | collective-permute-start | bytes 196616 | tf_op jit(solution)/shard_map/ppermute | solution.py:19
  171.9 13.5 %copy-start.16 = (bf16[256,512]{1,0:T(8,128)(2,1)}, bf16[256,512]{1,0:T(8,128)(2,1)S(1)}, u32[]{:S(2)}) copy-start(bf16[256,512]{1,0:T(8,128)(2,1)S(1)} %fusion.67) | copy-start | bytes 786436
  172.3 4.3 %collective-permute-start.10 = (bf16[1,128,512]{2,1,0:T(8,128)(2,1)S(1)}, bf16[1,128,512]{2,1,0:T(8,128)(2,1)S(1)}, u32[]{:S(2)}, u32[]{:S(2)}) collective-permute-start(bf16[1,128,512]{2,1,0:T(8,128)(2,1)S(1)} %get-tuple-element.61), channel_id=1, source_target_pairs={{0,1},{1,2},{2,3},{3,4},{4,5},{5,6},{6,7},{7,8},{8,9},{9,10},{10,1... | collective-permute-start | bytes 393224 | tf_op jit(solution)/shard_map/ppermute | solution.py:17
  174.2 7.2 %collective-permute-start.11 = (bf16[1,128,512]{2,1,0:T(8,128)(2,1)S(1)}, bf16[1,128,512]{2,1,0:T(8,128)(2,1)S(1)}, u32[]{:S(2)}, u32[]{:S(2)}) collective-permute-start(bf16[1,128,512]{2,1,0:T(8,128)(2,1)S(1)} %get-tuple-element.62), channel_id=1, source_target_pairs={{1,0},{2,1},{3,2},{4,3},{5,4},{6,5},{7,6},{8,7},{9,8},{10,9},{11,1... | collective-permute-start | bytes 393224 | tf_op jit(solution)/shard_map/ppermute | solution.py:19
Sparse Core Ops, SparseCore 0:
  110.2 36.9 all-gather.1
where the time goes:
time: 198 us; the launch traced here: 197 us
  waiting for transfers between devices  60.4 us (31%)
  local copies, waits for them, and re-layouts  54.7 us (28%)
  matrix products  36.1 us (18%)
  starting transfers between devices  28.6 us (14%)
  between operations  14.9 us (8%)
    gather x12, local copies, waits for them, and re-layouts, process_local(): fetched = extended[local_ids[:, slot_index]].astype(jnp.float32)  40.9 us
    all_gather x1, waiting for transfers between devices, local(): fragment = lax.all_gather(peer_proj, 'tile', axis=0, tiled=True)  36.7 us
    ppermute x6, waiting for transfers between devices, with_halo(): lax.ppermute(head, axis, [((i + 1) % count, i) for i in range(ends)])  23.7 us
    ppermute x6, starting transfers between devices, with_halo(): lax.ppermute(tail, axis, [(i, (i + 1) % count) for i in range(ends)])  14.9 us
    ppermute x6, starting transfers between devices, with_halo(): lax.ppermute(head, axis, [((i + 1) % count, i) for i in range(ends)])  13.6 us
    dot_general x1, matrix products, finish_level(): jnp.dot(message, node_message[level_index], preferred_element_type=jnp.fl...  9.98 us
    gather x6, local copies, waits for them, and re-layouts, local(): fragment[jnp.clip(where_ids, 0, row_count - 1)].astype(jnp.float32)  8.41 us
    dot_general x3, matrix products, finish_level(): jnp.dot(hidden, node_out[level_index], preferred_element_type=jnp.float32)  6.61 us
  transfers between devices with their start and end apart: 13, of which 7 were waited for; matrix products, arithmetic and copies ran while one was open for 3% of the time, Pallas kernels for 0%

commit v1 on v0

--- a/solution.py
+++ b/solution.py
@@ -4,6 +4,18 @@
 from jax.sharding import PartitionSpec as P
 
 COLS = 256
+
+
+def doubled_up(value, axis, dim):
+    ways, here = (lax.axis_size(axis), lax.axis_index(axis))
+    grown, reach = (value, 1)
+    while reach < ways:
+        theirs = lax.ppermute(grown, axis, [(d, d ^ reach) for d in range(ways)])
+        mine_first = jnp.concatenate([grown, theirs], axis=dim)
+        theirs_first = jnp.concatenate([theirs, grown], axis=dim)
+        grown = jnp.where(here & reach == 0, mine_first, theirs_first)
+        reach = 2 * reach
+    return grown
 
 
 def with_halo(cells, sides, width):
@@ -150,7 +162,7 @@
         coarse_table, lax.axis_index("tile") * coarse_count, coarse_count, 0
     )
     running = jnp.zeros(own_proj.shape, jnp.float32)
-    fragment = lax.all_gather(peer_proj, "tile", axis=0, tiled=True)
+    fragment = doubled_up(peer_proj, "tile", 0)
     row_count = fragment.shape[0]
     for slot_index in range(6):
         where_ids = my_table[:, slot_index]

time: 198 us -> 180 us (0.909)
  between operations: 14.9 us -> 1.52 us
  waiting for transfers between devices: 60.4 us -> 55.8 us
  local copies, waits for them, and re-layouts: 54.7 us -> 50.7 us
  starting transfers between devices: 28.6 us -> 32.6 us
    all_gather x1 -> x0, waiting for transfers between devices: 36.7 us -> none  [local(): fragment = lax.all_gather(peer_proj, 'tile', axis=0, tiled=True)]
    ppermute x0 -> x4, waiting for transfers between devices: none -> 32.8 us  [doubled_up(): theirs = lax.ppermute(grown, axis, [(d, d ^ reach) for d in range(ways)])]
    gather x6, local copies, waits for them, and re-layouts: 8.41 us -> 4.21 us  [local(): fragment[jnp.clip(where_ids, 0, row_count - 1)].astype(jnp.float32)]
    ppermute x0 -> x4, starting transfers between devices: none -> 3.88 us  [doubled_up(): theirs = lax.ppermute(grown, axis, [(d, d ^ reach) for d in range(ways)])]
  transfers between devices with their start and end apart: 13 -> 16, of which waited for: 7 -> 10; matrix products, arithmetic and copies ran while one was open for 3% -> 4% of each run, Pallas kernels for 0% -> 0%
where the time goes in v1:
time: 180 us; the launch traced here: 179 us
  waiting for transfers between devices  55.8 us (31%)
  local copies, waits for them, and re-layouts  50.7 us (28%)
  matrix products  35.4 us (20%)
  starting transfers between devices  32.6 us (18%)
  other arithmetic  2.63 us (1%)
    gather x12, local copies, waits for them, and re-layouts, process_local(): fetched = extended[local_ids[:, slot_index]].astype(jnp.float32)  40.8 us
    ppermute x4, waiting for transfers between devices, doubled_up(): theirs = lax.ppermute(grown, axis, [(d, d ^ reach) for d in range(ways)])  32.8 us
    ppermute x6, waiting for transfers between devices, with_halo(): lax.ppermute(head, axis, [((i + 1) % count, i) for i in range(ends)])  23 us
    ppermute x6, starting transfers between devices, with_halo(): lax.ppermute(tail, axis, [(i, (i + 1) % count) for i in range(ends)])  14.4 us
    ppermute x6, starting transfers between devices, with_halo(): lax.ppermute(head, axis, [((i + 1) % count, i) for i in range(ends)])  14.3 us
    dot_general x1, matrix products, finish_level(): jnp.dot(message, node_message[level_index], preferred_element_type=jnp.fl...  9.97 us
    dot_general x3, matrix products, finish_level(): jnp.dot(hidden, node_out[level_index], preferred_element_type=jnp.float32)  6.99 us
    dot_general x2, matrix products, descend_local(): jnp.dot(hidden, down_out[level_index], preferred_element_type=jnp.float32)  6.01 us
  transfers between devices with their start and end apart: 16, of which 10 were waited for; matrix products, arithmetic and copies ran while one was open for 4% of the time, Pallas kernels for 0%

profile of v1, /device:TPU:5, one launch (start us, length us, event | category | flops | bytes accessed | tf_op | source)
XLA Modules:
  0.0 178.6 jit_solution(2586097436608066798)
XLA Ops:
  0.7 2.1 %convolution_convert_fusion = bf16[1024,512]{1,0:T(8,128)(2,1)S(1)} fusion(bf16[1024,512]{1,0:T(8,128)(2,1)} %param.26, bf16[3,512,512]{2,1,0:T(8,128)(2,1)} %param.33), kind=kOutput, calls=%fused_computation.97 | convolution fusion | flops 537395200 | bytes 2621440 | tf_op jit(solution)/shard_map/dot_general | solution.py:76
  2.9 3.8 %collective-permute-start = (bf16[1,256,512]{2,1,0:T(8,128)(2,1)S(1)}, bf16[1,256,512]{2,1,0:T(8,128)(2,1)S(1)}, u32[]{:S(2)}, u32[]{:S(2)}) collective-permute-start(bf16[1,256,512]{2,1,0:T(8,128)(2,1)S(1)} %get-tuple-element.57), channel_id=1, source_target_pairs={{0,1},{1,2},{2,3},{3,4},{4,5},{5,6},{6,7},{7,8},{8,9},{9,10},{10,1... | collective-permute-start | bytes 786440 | tf_op jit(solution)/shard_map/ppermute | solution.py:29
  6.8 1.9 %collective-permute-start.1 = (bf16[1,256,512]{2,1,0:T(8,128)(2,1)S(1)}, bf16[1,256,512]{2,1,0:T(8,128)(2,1)S(1)}, u32[]{:S(2)}, u32[]{:S(2)}) collective-permute-start(bf16[1,256,512]{2,1,0:T(8,128)(2,1)S(1)} %get-tuple-element.58), channel_id=1, source_target_pairs={{1,0},{2,1},{3,2},{4,3},{5,4},{6,5},{7,6},{8,7},{9,8},{10,9},{11,1... | collective-permute-start | bytes 786440 | tf_op jit(solution)/shard_map/ppermute | solution.py:31
  8.9 3.1 %fusion.175 = f32[1024,512]{1,0:T(8,128)} fusion(bf16[1024,512]{1,0:T(8,128)(2,1)S(1)} %copy-done.2, bf16[3,512,512]{2,1,0:T(8,128)(2,1)} %param.35), kind=kOutput, calls=%fused_computation.223 | convolution fusion | flops 536870912 | bytes 3670016 | tf_op jit(solution)/shard_map/dot_general | solution.py:55
  12.2 3.2 %collective-permute-done.1 = bf16[1,256,512]{2,1,0:T(8,128)(2,1)S(1)} collective-permute-done((bf16[1,256,512]{2,1,0:T(8,128)(2,1)S(1)}, bf16[1,256,512]{2,1,0:T(8,128)(2,1)S(1)}, u32[]{:S(2)}, u32[]{:S(2)}) %collective-permute-start.1) | collective-permute-done | bytes 262176 | tf_op jit(solution)/shard_map/ppermute | solution.py:31
  15.6 5.1 %gather_fusion = bf16[1024,512]{1,0:T(8,128)(2,1)} fusion(bf16[1536,512]{1,0:T(8,128)(2,1)S(1)} %bitcast.196, s32[1024]{0:T(1024)S(1)} %broadcast_clamp_fusion.5), kind=kCustom, calls=%fused_computation | custom fusion | bytes 2101248 | tf_op jit(solution)/shard_map/gather | solution.py:88
  20.6 5.0 %gather_fusion.1 = bf16[1024,512]{1,0:T(8,128)(2,1)} fusion(bf16[1536,512]{1,0:T(8,128)(2,1)S(1)} %bitcast.197, s32[1024]{0:T(1024)S(1)} %broadcast_clamp_fusion.4), kind=kCustom, calls=%fused_computation.1 | custom fusion | bytes 2101248 | tf_op jit(solution)/shard_map/gather | solution.py:88
  25.7 5.1 %gather_fusion.2 = bf16[1024,512]{1,0:T(8,128)(2,1)} fusion(bf16[1536,512]{1,0:T(8,128)(2,1)S(1)} %bitcast.198, s32[1024]{0:T(1024)S(1)} %broadcast_clamp_fusion.3), kind=kCustom, calls=%fused_computation.2 | custom fusion | bytes 2101248 | tf_op jit(solution)/shard_map/gather | solution.py:88
  30.7 5.1 %gather_fusion.3 = bf16[1024,512]{1,0:T(8,128)(2,1)} fusion(bf16[1536,512]{1,0:T(8,128)(2,1)S(1)} %bitcast.199, s32[1024]{0:T(1024)S(1)} %broadcast_clamp_fusion.2), kind=kCustom, calls=%fused_computation.3 | custom fusion | bytes 2101248 | tf_op jit(solution)/shard_map/gather | solution.py:88
  35.8 5.1 %gather_fusion.4 = bf16[1024,512]{1,0:T(8,128)(2,1)} fusion(bf16[1536,512]{1,0:T(8,128)(2,1)S(1)} %bitcast.200, s32[1024]{0:T(1024)S(1)} %broadcast_clamp_fusion.1), kind=kCustom, calls=%fused_computation.4 | custom fusion | bytes 2101248 | tf_op jit(solution)/shard_map/gather | solution.py:88
  40.8 5.1 %gather_fusion.5 = bf16[1024,512]{1,0:T(8,128)(2,1)} fusion(bf16[1536,512]{1,0:T(8,128)(2,1)S(1)} %bitcast.201, s32[1024]{0:T(1024)S(1)} %broadcast_clamp_fusion), kind=kCustom, calls=%fused_computation.5 | custom fusion | bytes 2101248 | tf_op jit(solution)/shard_map/gather | solution.py:88
  45.9 10.0 %fusion.54 = bf16[1024,512]{1,0:T(8,128)(2,1)S(1)} fusion(f32[1024,512]{1,0:T(8,128)} %fusion.175, f32[512]{0:T(512)S(1)} %bitcast.241, bf16[1024,512]{1,0:T(8,128)(2,1)} %gather_fusion.5, bf16[1024,512]{1,0:T(8,128)(2,1)} %gather_fusion.4, bf16[1024,512]{1,0:T(8,128)(2,1)} %gather_fusion.3, bf16[1024,512]{1,0:T(8,128)(2,1)} %gather_fusion.2, ...), kind=kOutput, calls=%fused_computation.82 | convolution fusion | flops 1114636288 | bytes 11538432 | tf_op jit(solution)/shard_map/dot_general | solution.py:58
  55.9 1.7 add_convert_fusion.1
  57.7 0.7 fusion.365
  58.4 0.2 copy-done.18
  58.6 1.9 %collective-permute-start.2 = (bf16[1,128,512]{2,1,0:T(8,128)(2,1)S(1)}, bf16[1,128,512]{2,1,0:T(8,128)(2,1)S(1)}, u32[]{:S(2)}, u32[]{:S(2)}) collective-permute-start(bf16[1,128,512]{2,1,0:T(8,128)(2,1)S(1)} %get-tuple-element.59), channel_id=1, source_target_pairs={{0,1},{1,2},{2,3},{3,4},{4,5},{5,6},{6,7},{7,8},{8,9},{9,10},{10,1... | collective-permute-start | bytes 393224 | tf_op jit(solution)/shard_map/ppermute | solution.py:29
  60.6 2.6 %collective-permute-start.3 = (bf16[1,128,512]{2,1,0:T(8,128)(2,1)S(1)}, bf16[1,128,512]{2,1,0:T(8,128)(2,1)S(1)}, u32[]{:S(2)}, u32[]{:S(2)}) collective-permute-start(bf16[1,128,512]{2,1,0:T(8,128)(2,1)S(1)} %get-tuple-element.60), channel_id=1, source_target_pairs={{1,0},{2,1},{3,2},{4,3},{5,4},{6,5},{7,6},{8,7},{9,8},{10,9},{11,1... | collective-permute-start | bytes 393224 | tf_op jit(solution)/shard_map/ppermute | solution.py:31
  63.2 4.5 %collective-permute-done.3 = bf16[1,128,512]{2,1,0:T(8,128)(2,1)S(1)} collective-permute-done((bf16[1,128,512]{2,1,0:T(8,128)(2,1)S(1)}, bf16[1,128,512]{2,1,0:T(8,128)(2,1)S(1)}, u32[]{:S(2)}, u32[]{:S(2)}) %collective-permute-start.3) | collective-permute-done | bytes 131104 | tf_op jit(solution)/shard_map/ppermute | solution.py:31
  68.1 1.5 convolution_convert_fusion.2
  69.6 0.3 fusion.160
  69.9 1.9 %collective-permute-start.4 = (bf16[1,128,512]{2,1,0:T(8,128)(2,1)S(1)}, bf16[1,128,512]{2,1,0:T(8,128)(2,1)S(1)}, u32[]{:S(2)}, u32[]{:S(2)}) collective-permute-start(bf16[1,128,512]{2,1,0:T(8,128)(2,1)S(1)} %get-tuple-element.63), channel_id=1, source_target_pairs={{0,1},{1,2},{2,3},{3,4},{4,5},{5,6},{6,7},{7,8},{8,9},{9,10},{10,1... | collective-permute-start | bytes 393224 | tf_op jit(solution)/shard_map/ppermute | solution.py:29
  71.9 2.4 %collective-permute-start.5 = (bf16[1,128,512]{2,1,0:T(8,128)(2,1)S(1)}, bf16[1,128,512]{2,1,0:T(8,128)(2,1)S(1)}, u32[]{:S(2)}, u32[]{:S(2)}) collective-permute-start(bf16[1,128,512]{2,1,0:T(8,128)(2,1)S(1)} %get-tuple-element.64), channel_id=1, source_target_pairs={{1,0},{2,1},{3,2},{4,3},{5,4},{6,5},{7,6},{8,7},{9,8},{10,9},{11,1... | collective-permute-start | bytes 393224 | tf_op jit(solution)/shard_map/ppermute | solution.py:31
  74.3 1.3 convolution_add_fusion.3
  75.6 0.8 fusion.163
  76.4 2.6 %collective-permute-done.5 = bf16[1,128,512]{2,1,0:T(8,128)(2,1)S(1)} collective-permute-done((bf16[1,128,512]{2,1,0:T(8,128)(2,1)S(1)}, bf16[1,128,512]{2,1,0:T(8,128)(2,1)S(1)}, u32[]{:S(2)}, u32[]{:S(2)}) %collective-permute-start.5) | collective-permute-done | bytes 131104 | tf_op jit(solution)/shard_map/ppermute | solution.py:31
  79.1 1.2 gather_fusion.10
  80.3 1.8 %gather_fusion.6 = bf16[256,512]{1,0:T(8,128)(2,1)} fusion(bf16[512,512]{1,0:T(8,128)(2,1)S(1)} %bitcast.203, s32[1024]{0:T(1024)S(1)} %pad_clamp_fusion.12), kind=kCustom, calls=%fused_computation.6 | custom fusion | bytes 525312 | tf_op jit(solution)/shard_map/gather | solution.py:88
  82.1 1.8 %gather_fusion.7 = bf16[256,512]{1,0:T(8,128)(2,1)} fusion(bf16[512,512]{1,0:T(8,128)(2,1)S(1)} %bitcast.204, s32[1024]{0:T(1024)S(1)} %pad_clamp_fusion.11), kind=kCustom, calls=%fused_computation.7 | custom fusion | bytes 525312 | tf_op jit(solution)/shard_map/gather | solution.py:88
  84.0 1.9 %gather_fusion.8 = bf16[256,512]{1,0:T(8,128)(2,1)} fusion(bf16[512,512]{1,0:T(8,128)(2,1)S(1)} %bitcast.205, s32[1024]{0:T(1024)S(1)} %pad_clamp_fusion.10), kind=kCustom, calls=%fused_computation.8 | custom fusion | bytes 525312 | tf_op jit(solution)/shard_map/gather | solution.py:88
  85.8 1.9 %gather_fusion.9 = bf16[256,512]{1,0:T(8,128)(2,1)} fusion(bf16[512,512]{1,0:T(8,128)(2,1)S(1)} %bitcast.206, s32[1024]{0:T(1024)S(1)} %pad_clamp_fusion.9), kind=kCustom, calls=%fused_computation.9 | custom fusion | bytes 525312 | tf_op jit(solution)/shard_map/gather | solution.py:88
  87.7 1.9 %gather_fusion.11 = bf16[256,512]{1,0:T(8,128)(2,1)} fusion(bf16[512,512]{1,0:T(8,128)(2,1)S(1)} %bitcast.207, s32[1024]{0:T(1024)S(1)} %pad_clamp_fusion.7), kind=kCustom, calls=%fused_computation.11 | custom fusion | bytes 525312 | tf_op jit(solution)/shard_map/gather | solution.py:88
  89.5 3.3 %fusion.66 = bf16[256,512]{1,0:T(8,128)(2,1)S(1)} fusion(f32[256,512]{1,0:T(8,128)S(1)} %fusion.160, bf16[3,512,512]{2,1,0:T(8,128)(2,1)} %param.38, bf16[3,512,512]{2,1,0:T(8,128)(2,1)} %param.36, bf16[256,512]{1,0:T(8,128)(2,1)} %fusion.163, f32[256,512]{1,0:T(8,128)S(1)} %convolution_add_fusion.3, bf16[256,512]{1,0:T(8,128)(2,1)} %gather_fusion.11, ...), kind=kOutput, calls=%fused_computation.103 | convolution fusion | flops 278921216 | bytes 4196352 | tf_op jit(solution)/shard_map/dot_general | solution.py:62
  92.8 0.2 fusion.366
  93.1 1.9 %collective-permute-start.6 = (bf16[1,64,512]{2,1,0:T(8,128)(2,1)S(1)}, bf16[1,64,512]{2,1,0:T(8,128)(2,1)S(1)}, u32[]{:S(2)}, u32[]{:S(2)}) collective-permute-start(bf16[1,64,512]{2,1,0:T(8,128)(2,1)S(1)} %get-tuple-element.65), channel_id=1, source_target_pairs={{0,1},{1,2},{2,3},{3,4},{4,5},{5,6},{6,7},{7,8},{8,9},{9,10},{10,1... | collective-permute-start | bytes 196616 | tf_op jit(solution)/shard_map/ppermute | solution.py:29
  95.0 2.4 %collective-permute-start.7 = (bf16[1,64,512]{2,1,0:T(8,128)(2,1)S(1)}, bf16[1,64,512]{2,1,0:T(8,128)(2,1)S(1)}, u32[]{:S(2)}, u32[]{:S(2)}) collective-permute-start(bf16[1,64,512]{2,1,0:T(8,128)(2,1)S(1)} %get-tuple-element.66), channel_id=1, source_target_pairs={{1,0},{2,1},{3,2},{4,3},{5,4},{6,5},{7,6},{8,7},{9,8},{10,9},{11,1... | collective-permute-start | bytes 196616 | tf_op jit(solution)/shard_map/ppermute | solution.py:31
  97.5 4.0 %collective-permute-done.7 = bf16[1,64,512]{2,1,0:T(8,128)(2,1)S(1)} collective-permute-done((bf16[1,64,512]{2,1,0:T(8,128)(2,1)S(1)}, bf16[1,64,512]{2,1,0:T(8,128)(2,1)S(1)}, u32[]{:S(2)}, u32[]{:S(2)}) %collective-permute-start.7) | collective-permute-done | bytes 65568 | tf_op jit(solution)/shard_map/ppermute | solution.py:31
  101.7 1.2 convolution_convert_fusion.4
  103.1 1.2 collective-permute-done.8
  104.4 4.8 %collective-permute-done.9 = bf16[128,512]{1,0:T(8,128)(2,1)S(1)} collective-permute-done((bf16[128,512]{1,0:T(8,128)(2,1)S(1)}, bf16[128,512]{1,0:T(8,128)(2,1)S(1)}, u32[]{:S(2)}, u32[]{:S(2)}) %collective-permute-start.9) | collective-permute-done | bytes 131104 | tf_op jit(solution)/shard_map/ppermute | solution.py:13
  109.3 1.4 collective-permute-start.10
  110.7 5.5 %collective-permute-done.10 = bf16[256,512]{1,0:T(8,128)(2,1)S(1)} collective-permute-done((bf16[256,512]{1,0:T(8,128)(2,1)S(1)}, bf16[256,512]{1,0:T(8,128)(2,1)S(1)}, u32[]{:S(2)}, u32[]{:S(2)}) %collective-permute-start.10) | collective-permute-done | bytes 262176 | tf_op jit(solution)/shard_map/ppermute | solution.py:13
  116.3 0.2 maximum_select_fusion.1
  116.5 2.4 %collective-permute-start.11 = (bf16[512,512]{1,0:T(8,128)(2,1)S(1)}, bf16[512,512]{1,0:T(8,128)(2,1)S(1)}, u32[]{:S(2)}, u32[]{:S(2)}) collective-permute-start(bf16[512,512]{1,0:T(8,128)(2,1)S(1)} %maximum_select_fusion.1), channel_id=1, source_target_pairs={{0,8},{1,9},{2,10},{3,11},{4,12},{5,13},{6,14},{7,15},{8,0},{9,1},... | collective-permute-start | bytes 1572872 | tf_op jit(solution)/shard_map/ppermute | solution.py:13
  119.1 1.2 convolution_add_fusion.6
  120.3 21.2 %collective-permute-done.11 = bf16[512,512]{1,0:T(8,128)(2,1)S(1)} collective-permute-done((bf16[512,512]{1,0:T(8,128)(2,1)S(1)}, bf16[512,512]{1,0:T(8,128)(2,1)S(1)}, u32[]{:S(2)}, u32[]{:S(2)}) %collective-permute-start.11) | collective-permute-done | bytes 524320 | tf_op jit(solution)/shard_map/ppermute | solution.py:13
  141.5 0.5 maximum_select_fusion
  142.0 0.7 gather_fusion.12
  142.7 0.7 gather_fusion.13
  143.4 0.7 gather_fusion.14
  144.1 0.7 gather_fusion.15
  144.8 0.7 gather_fusion.16
  145.5 0.7 gather_fusion.17
  146.2 2.0 %fusion.69 = bf16[64,512]{1,0:T(8,128)(2,1)S(1)} fusion(bf16[3,512,512]{2,1,0:T(8,128)(2,1)} %param.38, f32[64,512]{1,0:T(8,128)S(1)} %fusion.151, bf16[3,512,512]{2,1,0:T(8,128)(2,1)} %param.36, bf16[64,512]{1,0:T(8,128)(2,1)S(1)} %multiply_convert_fusion.1, f32[64,512]{1,0:T(8,128)S(1)} %convolution_add_fusion.6, bf16[64,512]{1,0:T(8,128)(2,1)S(1)} %gather_fusion.17, ...), kind=kOutput, calls=%fused_computation.111 | convolution fusion | flops 69926912 | bytes 1837440 | tf_op jit(solution)/shard_map/dot_general | solution.py:62
  148.4 2.9 %collective-permute-start.12 = (bf16[1,64,512]{2,1,0:T(8,128)(2,1)S(1)}, bf16[1,64,512]{2,1,0:T(8,128)(2,1)S(1)}, u32[]{:S(2)}, u32[]{:S(2)}) collective-permute-start(bf16[1,64,512]{2,1,0:T(8,128)(2,1)S(1)} %fusion.70), channel_id=1, source_target_pairs={{0,1},{1,2},{2,3},{3,4},{4,5},{5,6},{6,7},{7,8},{8,9},{9,10},{10,1... | collective-permute-start | bytes 196616 | tf_op jit(solution)/shard_map/ppermute | solution.py:29
  151.4 2.5 %collective-permute-start.13 = (bf16[1,64,512]{2,1,0:T(8,128)(2,1)S(1)}, bf16[1,64,512]{2,1,0:T(8,128)(2,1)S(1)}, u32[]{:S(2)}, u32[]{:S(2)}) collective-permute-start(bf16[1,64,512]{2,1,0:T(8,128)(2,1)S(1)} %fusion.70), channel_id=1, source_target_pairs={{1,0},{2,1},{3,2},{4,3},{5,4},{6,5},{7,6},{8,7},{9,8},{10,9},{11,1... | collective-permute-start | bytes 196616 | tf_op jit(solution)/shard_map/ppermute | solution.py:31
  153.9 3.9 %collective-permute-done.13 = bf16[1,64,512]{2,1,0:T(8,128)(2,1)S(1)} collective-permute-done((bf16[1,64,512]{2,1,0:T(8,128)(2,1)S(1)}, bf16[1,64,512]{2,1,0:T(8,128)(2,1)S(1)}, u32[]{:S(2)}, u32[]{:S(2)}) %collective-permute-start.13) | collective-permute-done | bytes 65568 | tf_op jit(solution)/shard_map/ppermute | solution.py:31
  157.9 1.2 gather_fusion.18
  159.1 1.7 fusion.67
  160.8 0.3 convolution_convert_fusion.1
  161.1 1.9 %collective-permute-start.14 = (bf16[1,128,512]{2,1,0:T(8,128)(2,1)S(1)}, bf16[1,128,512]{2,1,0:T(8,128)(2,1)S(1)}, u32[]{:S(2)}, u32[]{:S(2)}) collective-permute-start(bf16[1,128,512]{2,1,0:T(8,128)(2,1)S(1)} %get-tuple-element.61), channel_id=1, source_target_pairs={{0,1},{1,2},{2,3},{3,4},{4,5},{5,6},{6,7},{7,8},{8,9},{9,10},{10,1... | collective-permute-start | bytes 393224 | tf_op jit(solution)/shard_map/ppermute | solution.py:29
  163.0 2.4 %collective-permute-start.15 = (bf16[1,128,512]{2,1,0:T(8,128)(2,1)S(1)}, bf16[1,128,512]{2,1,0:T(8,128)(2,1)S(1)}, u32[]{:S(2)}, u32[]{:S(2)}) collective-permute-start(bf16[1,128,512]{2,1,0:T(8,128)(2,1)S(1)} %get-tuple-element.62), channel_id=1, source_target_pairs={{1,0},{2,1},{3,2},{4,3},{5,4},{6,5},{7,6},{8,7},{9,8},{10,9},{11,1... | collective-permute-start | bytes 393224 | tf_op jit(solution)/shard_map/ppermute | solution.py:31
  165.5 4.8 %collective-permute-done.15 = bf16[1,128,512]{2,1,0:T(8,128)(2,1)S(1)} collective-permute-done((bf16[1,128,512]{2,1,0:T(8,128)(2,1)S(1)}, bf16[1,128,512]{2,1,0:T(8,128)(2,1)S(1)}, u32[]{:S(2)}, u32[]{:S(2)}) %collective-permute-start.15) | collective-permute-done | bytes 131104 | tf_op jit(solution)/shard_map/ppermute | solution.py:31
  170.3 4.0 %gather_fusion.19 = bf16[1024,512]{1,0:T(8,128)(2,1)S(1)} fusion(bf16[512,512]{1,0:T(8,128)(2,1)S(1)} %bitcast.208, s32[1024]{0:T(1024)S(1)} %get-tuple-element.51), kind=kCustom, calls=%fused_computation.19 | custom fusion | bytes 2101248 | tf_op jit(solution)/shard_map/gather | solution.py:117
  174.3 4.3 %add_convert_fusion = bf16[1024,512]{1,0:T(8,128)(2,1)} fusion(bf16[1024,512]{1,0:T(8,128)(2,1)} %copy-done.18, bf16[1024,512]{1,0:T(8,128)(2,1)S(1)} %gather_fusion.19, f32[512]{0:T(512)S(1)} %bitcast.239, bf16[2,512,512]{2,1,0:T(8,128)(2,1)S(1)} %copy-done.16, bf16[2,512,512]{2,1,0:T(8,128)(2,1)} %param.40), kind=kOutput, calls=%fused_computation.91 | convolution fusion | flops 1081606144 | bytes 5244928 | tf_op jit(solution)/shard_map/dot_general | solution.py:124
  (96 shorter events, 2.1 us)
Async XLA Ops:
  0.6 96.8 %copy-start = (s32[1024,6]{0,1:T(8,128)S(1)}, s32[1024,6]{0,1:T(8,128)}, u32[]{:S(2)}) copy-start(s32[1024,6]{0,1:T(8,128)} %param.29) | copy-start | bytes 73732
  0.6 8.2 %copy-start.2 = (bf16[1024,512]{1,0:T(8,128)(2,1)S(1)}, bf16[1024,512]{1,0:T(8,128)(2,1)}, u32[]{:S(2)}) copy-start(bf16[1024,512]{1,0:T(8,128)(2,1)} %param.26) | copy-start | bytes 3145732
  0.7 8.1 %copy-start.8 = (s32[1024,6]{0,1:T(8,128)S(1)}, s32[1024,6]{0,1:T(8,128)}, u32[]{:S(2)}) copy-start(s32[1024,6]{0,1:T(8,128)} %param.27) | copy-start | bytes 73732
  0.7 8.2 %copy-start.10 = (f32[3,512]{1,0:T(4,128)S(1)}, f32[3,512]{1,0:T(4,128)}, u32[]{:S(2)}) copy-start(f32[3,512]{1,0:T(4,128)} %param.37) | copy-start | bytes 18436
  2.9 9.1 %copy-start.13 = (f32[2,512]{1,0:T(2,128)S(1)}, f32[2,512]{1,0:T(2,128)}, u32[]{:S(2)}) copy-start(f32[2,512]{1,0:T(2,128)} %param.39) | copy-start | bytes 12292
  2.9 9.1 %copy-start.12 = (s32[1024]{0:T(1024)S(1)}, s32[1024]{0:T(1024)}, u32[]{:S(2)}) copy-start(s32[1024]{0:T(1024)} %param.30) | copy-start | bytes 12292
  2.9 9.1 %copy-start.9 = (s32[256,6]{0,1:T(8,128)S(1)}, s32[256,6]{0,1:T(8,128)}, u32[]{:S(2)}) copy-start(s32[256,6]{0,1:T(8,128)} %param.28) | copy-start | bytes 18436
  2.9 9.2 %copy-start.15 = (s32[256]{0:T(256)S(1)}, s32[256]{0:T(256)}, u32[]{:S(2)}) copy-start(s32[256]{0:T(256)} %param.31) | copy-start | bytes 3076
  2.9 9.2 %copy-start.11 = (f32[3,512]{1,0:T(4,128)S(1)}, f32[3,512]{1,0:T(4,128)}, u32[]{:S(2)}) copy-start(f32[3,512]{1,0:T(4,128)} %param.34) | copy-start | bytes 18436
  2.9 9.2 %collective-permute-start = (bf16[1,256,512]{2,1,0:T(8,128)(2,1)S(1)}, bf16[1,256,512]{2,1,0:T(8,128)(2,1)S(1)}, u32[]{:S(2)}, u32[]{:S(2)}) collective-permute-start(bf16[1,256,512]{2,1,0:T(8,128)(2,1)S(1)} %get-tuple-element.57), channel_id=1, source_target_pairs={{0,1},{1,2},{2,3},{3,4},{4,5},{5,6},{6,7},{7,8},{8,9},{9,10},{10,1... | collective-permute-start | bytes 786440 | tf_op jit(solution)/shard_map/ppermute | solution.py:29
  6.8 8.6 %collective-permute-start.1 = (bf16[1,256,512]{2,1,0:T(8,128)(2,1)S(1)}, bf16[1,256,512]{2,1,0:T(8,128)(2,1)S(1)}, u32[]{:S(2)}, u32[]{:S(2)}) collective-permute-start(bf16[1,256,512]{2,1,0:T(8,128)(2,1)S(1)} %get-tuple-element.58), channel_id=1, source_target_pairs={{1,0},{2,1},{3,2},{4,3},{5,4},{6,5},{7,6},{8,7},{9,8},{10,9},{11,1... | collective-permute-start | bytes 786440 | tf_op jit(solution)/shard_map/ppermute | solution.py:31
  40.8 5.1 %copy-start.3 = (bf16[1024,512]{1,0:T(8,128)(2,1)S(1)}, bf16[1024,512]{1,0:T(8,128)(2,1)}, u32[]{:S(2)}) copy-start(bf16[1024,512]{1,0:T(8,128)(2,1)} %param.26) | copy-start | bytes 3145732
  57.6 1.0 copy-start.18
  58.6 4.6 %collective-permute-start.2 = (bf16[1,128,512]{2,1,0:T(8,128)(2,1)S(1)}, bf16[1,128,512]{2,1,0:T(8,128)(2,1)S(1)}, u32[]{:S(2)}, u32[]{:S(2)}) collective-permute-start(bf16[1,128,512]{2,1,0:T(8,128)(2,1)S(1)} %get-tuple-element.59), channel_id=1, source_target_pairs={{0,1},{1,2},{2,3},{3,4},{4,5},{5,6},{6,7},{7,8},{8,9},{9,10},{10,1... | collective-permute-start | bytes 393224 | tf_op jit(solution)/shard_map/ppermute | solution.py:29
  60.6 7.2 %collective-permute-start.3 = (bf16[1,128,512]{2,1,0:T(8,128)(2,1)S(1)}, bf16[1,128,512]{2,1,0:T(8,128)(2,1)S(1)}, u32[]{:S(2)}, u32[]{:S(2)}) collective-permute-start(bf16[1,128,512]{2,1,0:T(8,128)(2,1)S(1)} %get-tuple-element.60), channel_id=1, source_target_pairs={{1,0},{2,1},{3,2},{4,3},{5,4},{6,5},{7,6},{8,7},{9,8},{10,9},{11,1... | collective-permute-start | bytes 393224 | tf_op jit(solution)/shard_map/ppermute | solution.py:31
  67.8 1.8 %copy-start.1 = (bf16[3,512,512]{2,1,0:T(8,128)(2,1)S(1)}, bf16[3,512,512]{2,1,0:T(8,128)(2,1)}, u32[]{:S(2)}) copy-start(bf16[3,512,512]{2,1,0:T(8,128)(2,1)} %param.35) | copy-start | bytes 4718596
  69.9 6.5 %collective-permute-start.4 = (bf16[1,128,512]{2,1,0:T(8,128)(2,1)S(1)}, bf16[1,128,512]{2,1,0:T(8,128)(2,1)S(1)}, u32[]{:S(2)}, u32[]{:S(2)}) collective-permute-start(bf16[1,128,512]{2,1,0:T(8,128)(2,1)S(1)} %get-tuple-element.63), channel_id=1, source_target_pairs={{0,1},{1,2},{2,3},{3,4},{4,5},{5,6},{6,7},{7,8},{8,9},{9,10},{10,1... | collective-permute-start | bytes 393224 | tf_op jit(solution)/shard_map/ppermute | solution.py:29
  71.9 7.2 %collective-permute-start.5 = (bf16[1,128,512]{2,1,0:T(8,128)(2,1)S(1)}, bf16[1,128,512]{2,1,0:T(8,128)(2,1)S(1)}, u32[]{:S(2)}, u32[]{:S(2)}) collective-permute-start(bf16[1,128,512]{2,1,0:T(8,128)(2,1)S(1)} %get-tuple-element.64), channel_id=1, source_target_pairs={{1,0},{2,1},{3,2},{4,3},{5,4},{6,5},{7,6},{8,7},{9,8},{10,9},{11,1... | collective-permute-start | bytes 393224 | tf_op jit(solution)/shard_map/ppermute | solution.py:31
  92.8 8.7 %copy-start.5 = (bf16[256,512]{1,0:T(8,128)(2,1)}, bf16[256,512]{1,0:T(8,128)(2,1)S(1)}, u32[]{:S(2)}) copy-start(bf16[256,512]{1,0:T(8,128)(2,1)S(1)} %fusion.66) | copy-start | bytes 786436
  92.8 17.9 %copy-start.14 = (f32[2,512]{1,0:T(2,128)S(1)}, f32[2,512]{1,0:T(2,128)}, u32[]{:S(2)}) copy-start(f32[2,512]{1,0:T(2,128)} %param.42) | copy-start | bytes 12292
  93.1 4.4 %collective-permute-start.6 = (bf16[1,64,512]{2,1,0:T(8,128)(2,1)S(1)}, bf16[1,64,512]{2,1,0:T(8,128)(2,1)S(1)}, u32[]{:S(2)}, u32[]{:S(2)}) collective-permute-start(bf16[1,64,512]{2,1,0:T(8,128)(2,1)S(1)} %get-tuple-element.65), channel_id=1, source_target_pairs={{0,1},{1,2},{2,3},{3,4},{4,5},{5,6},{6,7},{7,8},{8,9},{9,10},{10,1... | collective-permute-start | bytes 196616 | tf_op jit(solution)/shard_map/ppermute | solution.py:29
  95.0 6.5 %collective-permute-start.7 = (bf16[1,64,512]{2,1,0:T(8,128)(2,1)S(1)}, bf16[1,64,512]{2,1,0:T(8,128)(2,1)S(1)}, u32[]{:S(2)}, u32[]{:S(2)}) collective-permute-start(bf16[1,64,512]{2,1,0:T(8,128)(2,1)S(1)} %get-tuple-element.66), channel_id=1, source_target_pairs={{1,0},{2,1},{3,2},{4,3},{5,4},{6,5},{7,6},{8,7},{9,8},{10,9},{11,1... | collective-permute-start | bytes 196616 | tf_op jit(solution)/shard_map/ppermute | solution.py:31
  103.0 1.3 collective-permute-start.8
  104.3 5.0 %collective-permute-start.9 = (bf16[128,512]{1,0:T(8,128)(2,1)S(1)}, bf16[128,512]{1,0:T(8,128)(2,1)S(1)}, u32[]{:S(2)}, u32[]{:S(2)}) collective-permute-start(bf16[128,512]{1,0:T(8,128)(2,1)S(1)} %maximum_select_fusion.3), channel_id=1, source_target_pairs={{0,2},{1,3},{2,0},{3,1},{4,6},{5,7},{6,4},{7,5},{8,10},{9,11},{10,... | collective-permute-start | bytes 393224 | tf_op jit(solution)/shard_map/ppermute | solution.py:13
  109.3 6.9 %collective-permute-start.10 = (bf16[256,512]{1,0:T(8,128)(2,1)S(1)}, bf16[256,512]{1,0:T(8,128)(2,1)S(1)}, u32[]{:S(2)}, u32[]{:S(2)}) collective-permute-start(bf16[256,512]{1,0:T(8,128)(2,1)S(1)} %maximum_select_fusion.2), channel_id=1, source_target_pairs={{0,4},{1,5},{2,6},{3,7},{4,0},{5,1},{6,2},{7,3},{8,12},{9,13},{10,... | collective-permute-start | bytes 786440 | tf_op jit(solution)/shard_map/ppermute | solution.py:13
  116.5 25.0 %collective-permute-start.11 = (bf16[512,512]{1,0:T(8,128)(2,1)S(1)}, bf16[512,512]{1,0:T(8,128)(2,1)S(1)}, u32[]{:S(2)}, u32[]{:S(2)}) collective-permute-start(bf16[512,512]{1,0:T(8,128)(2,1)S(1)} %maximum_select_fusion.1), channel_id=1, source_target_pairs={{0,8},{1,9},{2,10},{3,11},{4,12},{5,13},{6,14},{7,15},{8,0},{9,1},... | collective-permute-start | bytes 1572872 | tf_op jit(solution)/shard_map/ppermute | solution.py:13
  146.2 2.0 %copy-start.4 = (bf16[2,512,512]{2,1,0:T(8,128)(2,1)S(1)}, bf16[2,512,512]{2,1,0:T(8,128)(2,1)}, u32[]{:S(2)}) copy-start(bf16[2,512,512]{2,1,0:T(8,128)(2,1)} %param.41) | copy-start | bytes 3145732
  148.2 12.6 %copy-start.7 = (bf16[64,512]{1,0:T(8,128)(2,1)}, bf16[64,512]{1,0:T(8,128)(2,1)S(1)}, u32[]{:S(2)}) copy-start(bf16[64,512]{1,0:T(8,128)(2,1)S(1)} %fusion.69) | copy-start | bytes 196612
  148.2 10.8 %copy-start.6 = (bf16[256,512]{1,0:T(8,128)(2,1)S(1)}, bf16[256,512]{1,0:T(8,128)(2,1)}, u32[]{:S(2)}) copy-start(bf16[256,512]{1,0:T(8,128)(2,1)} %copy-done.5) | copy-start | bytes 786436
  148.2 10.8 %copy-start.16 = (bf16[2,512,512]{2,1,0:T(8,128)(2,1)S(1)}, bf16[2,512,512]{2,1,0:T(8,128)(2,1)}, u32[]{:S(2)}) copy-start(bf16[2,512,512]{2,1,0:T(8,128)(2,1)} %param.43) | copy-start | bytes 3145732
  148.4 5.5 %collective-permute-start.12 = (bf16[1,64,512]{2,1,0:T(8,128)(2,1)S(1)}, bf16[1,64,512]{2,1,0:T(8,128)(2,1)S(1)}, u32[]{:S(2)}, u32[]{:S(2)}) collective-permute-start(bf16[1,64,512]{2,1,0:T(8,128)(2,1)S(1)} %fusion.70), channel_id=1, source_target_pairs={{0,1},{1,2},{2,3},{3,4},{4,5},{5,6},{6,7},{7,8},{8,9},{9,10},{10,1... | collective-permute-start | bytes 196616 | tf_op jit(solution)/shard_map/ppermute | solution.py:29
  151.4 6.5 %collective-permute-start.13 = (bf16[1,64,512]{2,1,0:T(8,128)(2,1)S(1)}, bf16[1,64,512]{2,1,0:T(8,128)(2,1)S(1)}, u32[]{:S(2)}, u32[]{:S(2)}) collective-permute-start(bf16[1,64,512]{2,1,0:T(8,128)(2,1)S(1)} %fusion.70), channel_id=1, source_target_pairs={{1,0},{2,1},{3,2},{4,3},{5,4},{6,5},{7,6},{8,7},{9,8},{10,9},{11,1... | collective-permute-start | bytes 196616 | tf_op jit(solution)/shard_map/ppermute | solution.py:31
  160.8 13.5 %copy-start.17 = (bf16[256,512]{1,0:T(8,128)(2,1)}, bf16[256,512]{1,0:T(8,128)(2,1)S(1)}, u32[]{:S(2)}) copy-start(bf16[256,512]{1,0:T(8,128)(2,1)S(1)} %fusion.67) | copy-start | bytes 786436
  161.1 4.3 %collective-permute-start.14 = (bf16[1,128,512]{2,1,0:T(8,128)(2,1)S(1)}, bf16[1,128,512]{2,1,0:T(8,128)(2,1)S(1)}, u32[]{:S(2)}, u32[]{:S(2)}) collective-permute-start(bf16[1,128,512]{2,1,0:T(8,128)(2,1)S(1)} %get-tuple-element.61), channel_id=1, source_target_pairs={{0,1},{1,2},{2,3},{3,4},{4,5},{5,6},{6,7},{7,8},{8,9},{9,10},{10,1... | collective-permute-start | bytes 393224 | tf_op jit(solution)/shard_map/ppermute | solution.py:29
  163.0 7.2 %collective-permute-start.15 = (bf16[1,128,512]{2,1,0:T(8,128)(2,1)S(1)}, bf16[1,128,512]{2,1,0:T(8,128)(2,1)S(1)}, u32[]{:S(2)}, u32[]{:S(2)}) collective-permute-start(bf16[1,128,512]{2,1,0:T(8,128)(2,1)S(1)} %get-tuple-element.62), channel_id=1, source_target_pairs={{1,0},{2,1},{3,2},{4,3},{5,4},{6,5},{7,6},{8,7},{9,8},{10,9},{11,1... | collective-permute-start | bytes 393224 | tf_op jit(solution)/shard_map/ppermute | solution.py:31
